TPU v7x, 32 devices: a whole 2x2x4 slice. The times are simulated.
32 devices in a mesh: dp: 8 (over z, x), mp: 4 (over y, core).
Axes of the slice: x: 2, y: 2, z: 4, core: 2. Of those that a mesh axis runs over, the one named last changes fastest.
Arguments:
- features: bfloat16 [8192, 1024], P('dp'), may hold values from -6 to 6
- out_grads: bfloat16 [8192, 4, 1024], P('dp', None, 'mp'), may hold values from -0.0625 to 0.0625
- norm_grads: float32 [8, 2048], P('dp'), may hold values from -2 to 2
- owners: int32 [5], replicated, may hold values from 0 to 7, as said below
- moment1: float32 [4, 1024, 1024], P(None, 'dp', 'mp'), may hold values from -6 to 6
- moment2: float32 [4, 1024, 1024], P(None, 'dp', 'mp'), may hold values from 0.1 to 10
- left_stats: float32 [4, 1024, 1024], P(None, 'dp', 'mp'), may hold values from -1024 to 1024, as said below
- right_stats: float32 [4, 1024, 1024], P(None, 'dp', 'mp'), may hold values from -1024 to 1024, as said below
- left_basis: float32 [4, 1024, 1024], P(None, 'dp', 'mp'), may hold values from -1 to 2
- right_basis: float32 [4, 1024, 1024], P(None, 'dp', 'mp'), may hold values from -1 to 2
- norm_m: float32 [2048], P('dp'), may hold values from -6 to 6
- norm_v: float32 [2048], P('dp'), may hold values from 0.1 to 10
Outputs:
- new_moment1: float32 [4, 1024, 1024], P(None, 'dp', 'mp')
- new_moment2: float32 [4, 1024, 1024], P(None, 'dp', 'mp')
- new_left_stats: float32 [4, 1024, 1024], P(None, 'dp', 'mp')
- new_right_stats: float32 [4, 1024, 1024], P(None, 'dp', 'mp')
- new_left_basis: float32 [4, 1024, 1024], P(None, 'dp', 'mp')
- new_right_basis: float32 [4, 1024, 1024], P(None, 'dp', 'mp')
- update_slots: bfloat16 [8, 1024, 1024], P('dp', None, 'mp')
- new_norm_m: float32 [2048], P('dp')
- new_norm_v: float32 [2048], P('dp')
- norm_slots: float32 [8, 2048], P('dp')
Inputs may be any that keep to these rules, and one draw needn't show every extreme that they name: `owners`: the first 4 entries are distinct, so a dp index owns at most one tile; the last entry may equal any of them. `left_stats`: each tile of statistics is symmetric. `right_stats`: each tile of statistics is symmetric.
All inputs are finite; a program needn't handle non-finite values.
Results may differ from a plain program's by a relative error of at most 0.0072.
Values may be sent and summed in bfloat16 or wider, within the bound.
A program may use at most 128 MiB of HBM per device.

v0:
```python
import jax
import jax.numpy as jnp
from jax import lax
from jax.sharding import PartitionSpec as P

FIX_ONE = 1.0 - 0.9**10
FIX_TWO = 1.0 - 0.95**10
BF = jnp.bfloat16
F32 = jnp.float32


def contract(left, right, left_dim, right_dim):
    return lax.dot_general(
        left, right, (((left_dim,), (right_dim,)), ((), ())), preferred_element_type=F32
    )


def to_tile(blocks):
    out = lax.all_to_all(blocks, "mp", split_axis=1, concat_axis=1, tiled=True)
    k, n, r, c = out.shape
    return out.transpose(0, 2, 1, 3).reshape(k, r, n * c)


def to_home(rows, n):
    k, r, c = rows.shape
    out = rows.reshape(k, r, n, c // n).transpose(0, 2, 1, 3)
    return lax.all_to_all(out, "mp", split_axis=1, concat_axis=1, tiled=True)


def gather_rows(rows):
    return lax.all_gather(rows, "dp", axis=0, tiled=True)


def normalize(power):
    wide = power.astype(F32)
    return lax.rsqrt(jnp.sum(wide * wide, axis=0, keepdims=True) + 1e-06)


def shards(
    features,
    out_grads,
    norm_grads,
    owners,
    moment1,
    moment2,
    left_stats,
    right_stats,
    left_basis,
    right_basis,
    norm_m,
    norm_v,
):
    dp = lax.axis_size("dp")
    tiles, slab, width = moment1.shape
    full = slab * dp
    me = lax.axis_index("dp")
    row0 = me * slab
    narrow = to_tile(jnp.stack([left_basis, right_basis, left_stats, right_stats]).astype(BF))
    left_full = gather_rows(narrow[0])
    right_full = gather_rows(narrow[1])
    flat = out_grads.reshape(out_grads.shape[0], tiles * width)
    partial = contract(features, flat, 0, 0).astype(BF).reshape(dp, slab, tiles * width)
    parts = lax.all_to_all(partial, "dp", split_axis=0, concat_axis=0, tiled=True)
    grad_home = jnp.sum(parts.astype(F32), axis=0).astype(BF)
    grad_home = grad_home.reshape(slab, tiles, width).transpose(1, 0, 2)
    grad_rows = to_tile(grad_home[None])[0]
    grad_full = gather_rows(grad_rows)
    wide = to_tile(jnp.stack([moment1, moment2]))
    prod_l = contract(grad_rows, grad_full, 1, 1)
    grad_cols = lax.dynamic_slice_in_dim(grad_full, row0, slab, 1)
    prod_r = contract(grad_cols, grad_full, 0, 0)
    stats_l = (0.95 * narrow[2].astype(F32) + 0.05 * prod_l).astype(BF)
    stats_r = (0.95 * narrow[3].astype(F32) + 0.05 * prod_r).astype(BF)
    power_l = contract(stats_l, left_full, 1, 0).astype(BF)
    power_r = contract(stats_r, right_full, 1, 0).astype(BF)
    power_l_full = gather_rows(power_l)
    power_r_full = gather_rows(power_r)
    left_cols = lax.dynamic_slice_in_dim(left_full, row0, slab, 1)
    half = contract(left_cols, grad_full, 0, 0).astype(BF)
    rotated = contract(half, right_full, 1, 0)
    tile_one = 0.9 * wide[0] + 0.1 * rotated
    tile_two = 0.95 * wide[1] + 0.05 * rotated * rotated
    direction = (tile_one / FIX_ONE / (jnp.sqrt(tile_two / FIX_TWO) + 1e-08)).astype(BF)
    back = contract(direction, right_full, 1, 1).astype(BF)
    back_full = gather_rows(back)
    home1 = to_home(jnp.stack([rotated, prod_l, prod_r]).astype(BF), tiles).astype(F32)
    new_one = 0.9 * moment1 + 0.1 * home1[0]
    new_two = 0.95 * moment2 + 0.05 * home1[0] * home1[0]
    new_sl = 0.95 * left_stats + 0.05 * home1[1]
    new_sr = 0.95 * right_stats + 0.05 * home1[2]
    update = contract(narrow[0], back_full, 1, 0).astype(BF)

    def refine(power_full, power_rows):
        scale = normalize(power_full)
        iter_full = (power_full.astype(F32) * scale).astype(BF)
        iter_rows = (power_rows.astype(F32) * scale).astype(BF)
        gram = contract(iter_rows, iter_full, 1, 1).astype(BF)
        return 1.5 * iter_rows.astype(F32) - 0.5 * contract(gram, iter_full, 1, 0)

    new_l = refine(power_l_full, power_l)
    new_r = refine(power_r_full, power_r)
    home2 = to_home(jnp.stack([new_l.astype(BF), new_r.astype(BF), update]), tiles)
    new_bl = home2[0].astype(F32)
    new_br = home2[1].astype(F32)
    slot_of = jnp.arange(dp, dtype=jnp.int32)[:, None, None]
    slots = jnp.zeros((dp, slab, width), BF)
    for n in range(tiles):
        slots = jnp.where(slot_of == owners[n], home2[2, n][None], slots)
    update_slot = lax.all_to_all(slots, "dp", split_axis=0, concat_axis=0, tiled=True)
    update_slot = update_slot.reshape(1, full, width)
    norm_parts = norm_grads.reshape(dp, norm_m.shape[0])
    norm_parts = lax.all_to_all(norm_parts, "dp", split_axis=0, concat_axis=0, tiled=True)
    norm_total = jnp.sum(norm_parts, axis=0)
    new_nm = 0.9 * norm_m + 0.1 * norm_total
    new_nv = 0.95 * norm_v + 0.05 * norm_total * norm_total
    norm_step = new_nm / FIX_ONE / (jnp.sqrt(new_nv / FIX_TWO) + 1e-08)
    to_owner = (jnp.arange(dp, dtype=jnp.int32) == owners[tiles])[:, None]
    norm_out = jnp.where(to_owner, norm_step[None], 0.0)
    norm_slot = lax.all_to_all(norm_out, "dp", split_axis=0, concat_axis=0, tiled=True)
    norm_slot = norm_slot.reshape(1, -1)
    return (
        new_one,
        new_two,
        new_sl,
        new_sr,
        new_bl,
        new_br,
        update_slot,
        new_nm,
        new_nv,
        norm_slot,
    )


def solution(mesh):
    in_specs = (
        P("dp", None),
        P("dp", None, "mp"),
        P("dp", None),
        P(),
        P(None, "dp", "mp"),
        P(None, "dp", "mp"),
        P(None, "dp", "mp"),
        P(None, "dp", "mp"),
        P(None, "dp", "mp"),
        P(None, "dp", "mp"),
        P("dp"),
        P("dp"),
    )
    out_specs = (
        P(None, "dp", "mp"),
        P(None, "dp", "mp"),
        P(None, "dp", "mp"),
        P(None, "dp", "mp"),
        P(None, "dp", "mp"),
        P(None, "dp", "mp"),
        P("dp", None, "mp"),
        P("dp"),
        P("dp"),
        P("dp", None),
    )
    return jax.shard_map(shards, mesh=mesh, in_specs=in_specs, out_specs=out_specs, check_vma=False)
```

profile of v0, /device:TPU:0, one launch (start us, length us, event | category | flops | bytes accessed | tf_op | source)
XLA Modules:
  0.0 443.4 jit_solution(10692234722072050169)
XLA Ops:
  7.2 2.2 copy.122
  9.5 2.4 convolution_convert_fusion
  11.9 55.4 %all_to_all.50 = bf16[8,128,1024]{2,1,0:T(8,128)(2,1)} all-to-all(bf16[8,128,1024]{2,1,0:T(8,128)(2,1)S(1)} %bitcast.115), channel_id=1, replica_groups=mesh['dp'=8,'mp'=4] {'dp'}, dimensions={0} | all-to-all | bytes 4194304 | tf_op jit(solution)/shard_map/all_to_all | solution.py:63
  67.3 2.0 reduce_sum.39
  69.4 0.8 copy.97
  70.2 1.1 copy.98
  71.3 9.1 %all_to_all.51 = bf16[1,4,128,256]{3,2,0,1:T(8,128)(2,1)} all-to-all(bf16[1,4,128,256]{3,2,0,1:T(8,128)(2,1)S(1)} %copy.98), channel_id=1, replica_groups=mesh['dp'=8,'mp'=4] {'mp'}, dimensions={1} | all-to-all | bytes 524288 | tf_op jit(solution)/shard_map/all_to_all | solution.py:19
  80.4 1.8 copy.99
  82.6 1.2 copy.93
  83.8 1.2 copy.92
  85.2 16.9 %all_to_all.52 = bf16[4,4,128,256]{2,3,0,1:T(8,128)(2,1)S(1)} all-to-all(bf16[4,4,128,256]{2,3,0,1:T(8,128)(2,1)S(1)} %pad_maximum_fusion), channel_id=1, replica_groups=mesh['dp'=8,'mp'=4] {'mp'}, dimensions={1} | all-to-all | bytes 2097152 | tf_op jit(solution)/shard_map/all_to_all | solution.py:19
  102.1 0.8 fusion.83
  103.0 0.7 all-gather.7.cloned.1.call-update
  103.8 1.1 convert_multiply_fusion.5
  104.8 1.2 copy.117
  106.1 24.6 %all-gather.9.cloned.1.call-done = bf16[1024,1024]{0,1:T(8,128)(2,1)} async-done(((bf16[128,1024]{0,1:T(8,128)(2,1)}), bf16[1024,1024]{0,1:T(8,128)(2,1)}) %all-gather.9.cloned.1.call-update) | async-done | bytes 2097168 | tf_op jit(solution)/shard_map/all_gather | solution.py:31
  130.7 3.4 fusion.85
  134.1 47.8 %all-gather.11.cloned.1.call-done = bf16[1024,1024]{0,1:T(8,128)(2,1)} async-done(((bf16[128,1024]{0,1:T(8,128)(2,1)}), bf16[1024,1024]{0,1:T(8,128)(2,1)}) %all-gather.11.cloned.1.call-update) | async-done | bytes 2097168 | tf_op jit(solution)/shard_map/all_gather | solution.py:31
  181.8 3.3 convolution_convert_fusion.3
  185.3 0.2 copy.116
  185.5 2.8 fusion.86
  188.2 44.8 %all-gather.7.cloned.1.call-done = bf16[1024,1024]{0,1:T(8,128)(2,1)} async-done(((bf16[128,1024]{0,1:T(8,128)(2,1)}), bf16[1024,1024]{0,1:T(8,128)(2,1)}) %all-gather.7.cloned.1.call-update) | async-done | bytes 2097168 | tf_op jit(solution)/shard_map/all_gather | solution.py:31
  233.0 3.1 convolution_convert_fusion.4
  236.2 1.2 copy.108
  237.4 1.2 copy.109
  238.8 17.0 %all_to_all.53 = f32[2,4,128,256]{2,3,0,1:T(8,128)S(1)} all-to-all(f32[2,4,128,256]{2,3,0,1:T(8,128)S(1)} %pad_maximum_fusion.1), channel_id=1, replica_groups=mesh['dp'=8,'mp'=4] {'mp'}, dimensions={1} | all-to-all | bytes 2097152 | tf_op jit(solution)/shard_map/all_to_all | solution.py:19
  255.9 1.0 copy.118
  257.1 4.8 %fusion.87 = (bf16[128,1024]{1,0:T(8,128)(2,1)}, f32[128,1024]{1,0:T(8,128)}) fusion(bf16[1024,1024]{0,1:T(8,128)(2,1)} %all-gather.11.cloned.1.call-done, bf16[1024,1024]{0,1:T(8,128)(2,1)} %all-gather.9.cloned.1.call-done, bf16[1024,1024]{0,1:T(8,128)(2,1)} %all-gather.7.cloned.1.call-done, s32[]{:T(128)S(6)} %select_n.28), kind=kOutput, calls=%fused_computation.109 | convolution fusion | flops 537133056 | bytes 5242884 | tf_op jit(solution)/shard_map/dot_general | solution.py:13
  261.9 3.1 convolution_convert_fusion.2
  265.1 3.5 all-to-all-start.7
  268.6 0.7 fusion.84
  269.3 0.7 iota_compare_fusion
  269.9 5.2 %all-to-all-done.7 = f32[8,1,256]{2,1,0:T(1,128)S(1)} async-done(((f32[8,1,256]{2,1,0:T(1,128)}), f32[8,1,256]{2,1,0:T(1,128)S(1)}, u32[]{:S(2)}, u32[]{:S(2)}) %all-to-all-start.7) | async-done | bytes 8224 | tf_op jit(solution)/shard_map/all_to_all | solution.py:112
  275.2 0.6 add_divide_fusion
  275.8 0.7 broadcast_select_fusion
  276.4 3.5 all-to-all-start.8
  280.0 3.1 all-gather.15.cloned.1.call-done
  283.1 2.1 fusion.2
  285.1 3.5 fusion.24
  288.9 43.8 %all-gather.13.cloned.1.call-done = bf16[1024,1024]{1,0:T(8,128)(2,1)} async-done(((bf16[128,1024]{1,0:T(8,128)(2,1)}), bf16[1024,1024]{1,0:T(8,128)(2,1)}) %all-gather.13.cloned.1.call-update) | async-done | bytes 2097168 | tf_op jit(solution)/shard_map/all_gather | solution.py:31
  332.7 2.1 fusion
  334.8 3.5 fusion.27
  338.5 44.4 %all-gather.17.cloned.1.call-done = bf16[1024,1024]{1,0:T(8,128)(2,1)} async-done(((bf16[128,1024]{1,0:T(8,128)(2,1)}), bf16[1024,1024]{1,0:T(8,128)(2,1)}) %all-gather.17.cloned.1.call-update) | async-done | bytes 2097168 | tf_op jit(solution)/shard_map/all_gather | solution.py:31
  382.9 2.1 convolution_convert_fusion.1
  385.2 1.0 maximum_bitcast_fusion.1
  386.2 3.6 all-to-all-start.5
  389.8 1.8 stack.58
  391.6 1.7 copy.100
  393.3 0.9 stack.60
  394.2 1.7 copy.102
  396.1 2.0 maximum_bitcast_fusion
  398.1 3.3 all-to-all-done.5
  401.4 4.2 all-to-all-start.3
  405.6 1.3 iota_compare_fusion.1
  406.9 1.2 iota_compare_fusion.3
  408.1 1.1 select_select_fusion
  409.2 8.1 %all-to-all-done.3 = bf16[3,4,128,256]{3,2,0,1:T(8,128)(2,1)} async-done(((bf16[3,4,128,256]{3,2,0,1:T(8,128)(2,1)}), bf16[3,4,128,256]{3,2,0,1:T(8,128)(2,1)}, u32[]{:S(2)}, u32[]{:S(2)}) %all-to-all-start.3) | async-done | bytes 786464 | tf_op jit(solution)/shard_map/all_to_all | solution.py:27
  417.3 3.5 all-to-all-start.6
  420.8 1.4 convert_element_type.101
  422.5 1.5 fusion.48
  424.0 1.1 fusion.54
  425.1 10.1 %all-to-all-done.6 = bf16[8,128,256]{2,1,0:T(8,128)(2,1)S(1)} async-done(((bf16[8,128,256]{2,1,0:T(8,128)(2,1)}), bf16[8,128,256]{2,1,0:T(8,128)(2,1)S(1)}, u32[]{:S(2)}, u32[]{:S(2)}) %all-to-all-start.6) | async-done | bytes 524320 | tf_op jit(solution)/shard_map/all_to_all | solution.py:109
  435.1 0.8 copy.129
  435.9 0.6 copy.130
  (68 shorter events, 2.6 us)
Async XLA Ops:
  7.2 2.3 copy-start
  7.2 123.5 %all-gather.9.cloned.1.call-start = ((), (), s32[]{:S(2)}) async-start(), calls=%async_computation.10 | async-start | bytes 2359296 | tf_op jit(solution)/shard_map/all_gather | solution.py:31
  67.3 14.9 %copy-start.4 = (f32[4,128,256]{2,1,0:T(8,128)S(1)}, f32[4,128,256]{2,1,0:T(8,128)}, u32[]{:S(2)}) copy-start(f32[4,128,256]{2,1,0:T(8,128)} %param.19) | copy-start | bytes 1572868
  69.3 13.1 %copy-start.6 = (f32[4,128,256]{2,1,0:T(8,128)S(1)}, f32[4,128,256]{2,1,0:T(8,128)}, u32[]{:S(2)}) copy-start(f32[4,128,256]{2,1,0:T(8,128)} %param.18) | copy-start | bytes 1572868
  82.2 99.7 %all-gather.11.cloned.1.call-start = ((), (), s32[]{:S(2)}) async-start(), calls=%async_computation.11 | async-start | bytes 2359296 | tf_op jit(solution)/shard_map/all_gather | solution.py:31
  103.0 130.1 %all-gather.7.cloned.1.call-start = ((), (), s32[]{:S(2)}) async-start(), calls=%async_computation.9 | async-start | bytes 2359296 | tf_op jit(solution)/shard_map/all_gather | solution.py:31
  103.7 179.4 %all-gather.15.cloned.1.call-start = ((), (), s32[]{:S(2)}) async-start(), calls=%async_computation.13 | async-start | bytes 2359296 | tf_op jit(solution)/shard_map/all_gather | solution.py:31
  134.0 51.2 %copy-start.3 = (f32[1,128,4,256]{1,3,2,0:T(8,128)S(1)}, f32[1,128,4,256]{1,3,2,0:T(8,128)}, u32[]{:S(2)}) copy-start(f32[1,128,4,256]{1,3,2,0:T(8,128)} %get-tuple-element.17) | copy-start | bytes 1572868
  181.8 3.6 copy-start.1
  185.2 147.5 %all-gather.13.cloned.1.call-start = ((), (), s32[]{:S(2)}) async-start(), calls=%async_computation.12 | async-start | bytes 2359296 | tf_op jit(solution)/shard_map/all_gather | solution.py:31
  236.2 146.7 %all-gather.17.cloned.1.call-start = ((), (), s32[]{:S(2)}) async-start(), calls=%async_computation.14 | async-start | bytes 2359296 | tf_op jit(solution)/shard_map/all_gather | solution.py:31
  257.1 4.8 %copy-start.14 = (f32[128,1024]{1,0:T(8,128)S(1)}, f32[128,1024]{1,0:T(8,128)}, u32[]{:S(2)}) copy-start(f32[128,1024]{1,0:T(8,128)} %copy.118) | copy-start | bytes 1572868
  261.9 6.7 %copy-start.15 = (s32[5]{0:T(128)S(1)}, s32[5]{0:T(128)}, u32[]{:S(2)}) copy-start(s32[5]{0:T(128)} %param.15) | copy-start | bytes 64
  261.9 13.3 %copy-start.16 = (f32[256]{0:T(256)S(1)}, f32[256]{0:T(256)}, u32[]{:S(2)}) copy-start(f32[256]{0:T(256)} %param.23) | copy-start | bytes 3076
  261.9 13.3 %copy-start.17 = (f32[256]{0:T(256)S(1)}, f32[256]{0:T(256)}, u32[]{:S(2)}) copy-start(f32[256]{0:T(256)} %param.22) | copy-start | bytes 3076
  265.1 20.1 %copy-start.12 = (bf16[128,1024]{1,0:T(8,128)(2,1)S(1)}, bf16[128,1024]{1,0:T(8,128)(2,1)}, u32[]{:S(2)}) copy-start(bf16[128,1024]{1,0:T(8,128)(2,1)} %convolution_convert_fusion.3) | copy-start | bytes 786436
  265.1 10.1 %all-to-all-start.7 = ((f32[8,1,256]{2,1,0:T(1,128)}), f32[8,1,256]{2,1,0:T(1,128)S(1)}, u32[]{:S(2)}, u32[]{:S(2)}) async-start(f32[8,1,256]{2,1,0:T(1,128)} %bitcast.38), calls=%async_computation.7 | async-start | bytes 16384 | tf_op jit(solution)/shard_map/all_to_all | solution.py:112
  276.4 109.7 %all-to-all-start.8 = ((f32[8,1,256]{2,1,0:T(1,128)}), f32[8,1,256]{2,1,0:T(1,128)S(1)}, u32[]{:S(2)}, u32[]{:S(2)}) async-start(f32[8,1,256]{2,1,0:T(1,128)} %broadcast_select_fusion), calls=%async_computation.8 | async-start | bytes 16384 | tf_op jit(solution)/shard_map/all_to_all | solution.py:119
  288.6 46.1 %copy-start.13 = (bf16[128,1024]{1,0:T(8,128)(2,1)S(1)}, bf16[128,1024]{1,0:T(8,128)(2,1)}, u32[]{:S(2)}) copy-start(bf16[128,1024]{1,0:T(8,128)(2,1)} %convolution_convert_fusion.4) | copy-start | bytes 786436
  334.7 48.1 %copy-start.2 = (bf16[1,128,4,256]{1,3,2,0:T(8,128)(2,1)S(1)}, bf16[1,128,4,256]{1,3,2,0:T(8,128)(2,1)}, u32[]{:S(2)}) copy-start(bf16[1,128,4,256]{1,3,2,0:T(8,128)(2,1)} %get-tuple-element.21) | copy-start | bytes 786436
  385.2 8.2 %copy-start.10 = (bf16[128,1024]{1,0:T(8,128)(2,1)S(1)}, bf16[128,1024]{1,0:T(8,128)(2,1)}, u32[]{:S(2)}) copy-start(bf16[128,1024]{1,0:T(8,128)(2,1)} %get-tuple-element.34) | copy-start | bytes 786436
  386.2 9.7 %copy-start.11 = (bf16[128,1024]{1,0:T(8,128)(2,1)S(1)}, bf16[128,1024]{1,0:T(8,128)(2,1)}, u32[]{:S(2)}) copy-start(bf16[128,1024]{1,0:T(8,128)(2,1)} %get-tuple-element.36) | copy-start | bytes 786436
  386.2 15.2 %all-to-all-start.5 = ((bf16[3,4,128,256]{3,2,0,1:T(8,128)(2,1)}), bf16[3,4,128,256]{3,2,0,1:T(8,128)(2,1)S(1)}, u32[]{:S(2)}, u32[]{:S(2)}) async-start(bf16[3,4,128,256]{3,2,0,1:T(8,128)(2,1)} %maximum_bitcast_fusion.1), calls=%async_computation.5 | async-start | bytes 1572864 | tf_op jit(solution)/shard_map/all_to_all | solution.py:27
  401.4 15.9 %all-to-all-start.3 = ((bf16[3,4,128,256]{3,2,0,1:T(8,128)(2,1)}), bf16[3,4,128,256]{3,2,0,1:T(8,128)(2,1)}, u32[]{:S(2)}, u32[]{:S(2)}) async-start(bf16[3,4,128,256]{3,2,0,1:T(8,128)(2,1)} %maximum_bitcast_fusion), calls=%async_computation.3 | async-start | bytes 1572864 | tf_op jit(solution)/shard_map/all_to_all | solution.py:27
  417.3 17.9 %all-to-all-start.6 = ((bf16[8,128,256]{2,1,0:T(8,128)(2,1)}), bf16[8,128,256]{2,1,0:T(8,128)(2,1)S(1)}, u32[]{:S(2)}, u32[]{:S(2)}) async-start(bf16[8,128,256]{2,1,0:T(8,128)(2,1)} %select_select_fusion), calls=%async_computation.6 | async-start | bytes 1048576 | tf_op jit(solution)/shard_map/all_to_all | solution.py:109
  420.8 1.5 copy-start.5
  420.8 1.5 copy-start.7
  420.8 1.6 copy-start.8
  420.8 1.7 copy-start.9
Sparse Core Ops, SparseCore 0:
  82.3 48.3 all-gather.8
  133.3 48.5 all-gather.10
  184.5 48.5 all-gather.6
  235.6 47.4 all-gather.14
  285.0 47.5 all-gather.12
  335.2 47.6 all-gather.16
where the time goes:
time: 445 us; the launch traced here: 443 us
  waiting for transfers between devices  236 us (53%)
  blocking collectives  98.3 us (22%)
  matrix products  32 us (7%)
  local copies, waits for them, and re-layouts  24.2 us (5%)
  other arithmetic  20 us (4%)
  starting transfers between devices  18.5 us (4%)
  between operations  14.6 us (3%)
    all_gather x6, waiting for transfers between devices, gather_rows(): return lax.all_gather(rows, 'dp', axis=0, tiled=True)  208 us
    all_to_all x1, blocking collectives, shards(): lax.all_to_all(partial, 'dp', split_axis=0, concat_axis=0, tiled=True)  55.4 us
    all_to_all x3, blocking collectives, to_tile(): out = lax.all_to_all(blocks, 'mp', split_axis=1, concat_axis=1, tiled=True)  42.9 us
    dot_general x10, matrix products, contract(): lax.dot_general(left, right, (((left_dim,), (right_dim,)), ((), ())), pre...  32 us
    all_to_all x2, waiting for transfers between devices, to_home(): return lax.all_to_all(out, 'mp', split_axis=1, concat_axis=1, tiled=True)  11.3 us
    all_to_all x1, waiting for transfers between devices, shards(): lax.all_to_all(slots, 'dp', split_axis=0, concat_axis=0, tiled=True)  10.1 us
    unnamed x45, local copies, waits for them, and re-layouts  9.22 us
  transfers between devices with their start and end apart: 11, of which 10 were waited for; matrix products, arithmetic and copies ran while one was open for 14% of the time, Pallas kernels for 0%

commit v1 on v0

--- a/solution.py
+++ b/solution.py
@@ -1,3 +1,4 @@
+import functools
 import jax
 import jax.numpy as jnp
 from jax import lax
@@ -7,6 +8,17 @@
 FIX_TWO = 1.0 - 0.95**10
 BF = jnp.bfloat16
 F32 = jnp.float32
+
+
+def extend_node(z, a_name, array_dim):
+    ledger = []
+    for _ in range(lax.psum(1, a_name)):
+        ledger.append(z)
+    placed = jnp.concatenate(lax.all_to_all(jnp.stack(ledger, axis=0), a_name, 0, 0), array_dim)
+    return placed
+
+
+deliver_pairs_all = functools.partial(extend_node, a_name="dp", array_dim=0)
 
 
 def contract(left, right, left_dim, right_dim):
@@ -28,7 +40,7 @@
 
 
 def gather_rows(rows):
-    return lax.all_gather(rows, "dp", axis=0, tiled=True)
+    return deliver_pairs_all(rows)
 
 
 def normalize(power):

time: 445 us -> 511 us (1.15)
  waiting for transfers between devices: 236 us -> 354 us
  blocking collectives: 98.3 us -> 0 us
  starting transfers between devices: 18.5 us -> 64.1 us
  local copies, waits for them, and re-layouts: 24.2 us -> 41.7 us
  between operations: 14.6 us -> 1.08 us
  matrix products: 32 us -> 23.2 us
  other arithmetic: 20 us -> 25.4 us
    all_to_all x0 -> x10, waiting for transfers between devices: none -> 326 us  [the longest x6 256 us: extend_node(): lax.all_to_all(jnp.stack(ledger, axis=0), a_name, 0, 0)]
    all_gather x6 -> x0, waiting for transfers between devices: 208 us -> none  [gather_rows(): return lax.all_gather(rows, 'dp', axis=0, tiled=True)]
    all_to_all x4 -> x0, blocking collectives: 98.3 us -> none  [the longest x1 55.4 us: shards(): lax.all_to_all(partial, 'dp', split_axis=0, concat_axis=0, tiled=True)]
    all_to_all x0 -> x10, starting transfers between devices: none -> 43.7 us  [the longest x6 25.3 us: extend_node(): lax.all_to_all(jnp.stack(ledger, axis=0), a_name, 0, 0)]
    another operation x0 -> x7, local copies, waits for them, and re-layouts: none -> 12.8 us  [extend_node(): jnp.stack(ledger, axis=0)]
    dot_general x10, matrix products: 32 us -> 23.2 us  [contract(): lax.dot_general(left, right, (((left_dim,), (right_dim,)), ((), ())), pre...]
    all_to_all x2, waiting for transfers between devices: 11.3 us -> 17.9 us  [to_home(): return lax.all_to_all(out, 'mp', split_axis=1, concat_axis=1, tiled=True)]
    another operation x6, local copies, waits for them, and re-layouts: 6.29 us -> 0.63 us  [shards(): jnp.stack([rotated, prod_l, prod_r]).astype(BF)]
  transfers between devices with their start and end apart: 11 -> 15, of which waited for: 10 -> 13; matrix products, arithmetic and copies ran while one was open for 14% -> 13% of each run, Pallas kernels for 0% -> 0%
where the time goes in v1:
time: 511 us; the launch traced here: 509 us
  waiting for transfers between devices  354 us (69%)
  starting transfers between devices  64.1 us (13%)
  local copies, waits for them, and re-layouts  41.7 us (8%)
  other arithmetic  25.4 us (5%)
  matrix products  23.2 us (5%)
    all_to_all x6, waiting for transfers between devices, extend_node(): lax.all_to_all(jnp.stack(ledger, axis=0), a_name, 0, 0)  256 us
    all_to_all x1, waiting for transfers between devices, shards(): lax.all_to_all(partial, 'dp', split_axis=0, concat_axis=0, tiled=True)  44.4 us
    all_to_all x3, waiting for transfers between devices, to_tile(): out = lax.all_to_all(blocks, 'mp', split_axis=1, concat_axis=1, tiled=True)  25.5 us
    all_to_all x6, starting transfers between devices, extend_node(): lax.all_to_all(jnp.stack(ledger, axis=0), a_name, 0, 0)  25.3 us
    dot_general x10, matrix products, contract(): lax.dot_general(left, right, (((left_dim,), (right_dim,)), ((), ())), pre...  23.2 us
    all_to_all x2, waiting for transfers between devices, to_home(): return lax.all_to_all(out, 'mp', split_axis=1, concat_axis=1, tiled=True)  17.9 us
    unnamed x45, local copies, waits for them, and re-layouts  13.1 us
    another operation x7, local copies, waits for them, and re-layouts, extend_node(): jnp.stack(ledger, axis=0)  12.8 us
  transfers between devices with their start and end apart: 15, of which 13 were waited for; matrix products, arithmetic and copies ran while one was open for 13% of the time, Pallas kernels for 0%

profile of v1, /device:TPU:0, one launch (start us, length us, event | category | flops | bytes accessed | tf_op | source)
XLA Modules:
  0.0 509.4 jit_solution(16935816194279487394)
XLA Ops:
  0.7 1.4 copy.126
  2.0 1.2 copy.127
  3.3 1.2 copy.128
  5.3 2.0 pad_maximum_fusion
  7.4 4.3 all-to-all-start
  11.6 2.1 copy.159
  13.7 3.7 convolution_convert_fusion
  17.5 8.6 %all-to-all-done = bf16[4,4,128,256]{2,3,0,1:T(8,128)(2,1)S(1)} async-done(((bf16[4,4,128,256]{2,3,0,1:T(8,128)(2,1)}), bf16[4,4,128,256]{2,3,0,1:T(8,128)(2,1)S(1)}, u32[]{:S(2)}, u32[]{:S(2)}) %all-to-all-start) | async-done | bytes 1048608 | tf_op jit(solution)/shard_map/all_to_all | solution.py:31
  27.0 6.5 %all-to-all-start.2 = ((bf16[8,128,1024]{2,1,0:T(8,128)(2,1)}), bf16[8,128,1024]{2,1,0:T(8,128)(2,1)S(1)}, u32[]{:S(2)}, u32[]{:S(2)}) async-start(bf16[8,128,1024]{2,1,0:T(8,128)(2,1)} %bitcast.139), calls=%async_computation.2 | async-start | bytes 4194304 | tf_op jit(solution)/shard_map/all_to_all | solution.py:75
  33.6 1.2 copy.145
  34.8 1.2 copy.146
  37.1 44.4 %all-to-all-done.2 = bf16[8,128,1024]{2,1,0:T(8,128)(2,1)S(1)} async-done(((bf16[8,128,1024]{2,1,0:T(8,128)(2,1)}), bf16[8,128,1024]{2,1,0:T(8,128)(2,1)S(1)}, u32[]{:S(2)}, u32[]{:S(2)}) %all-to-all-start.2) | async-done | bytes 2097184 | tf_op jit(solution)/shard_map/all_to_all | solution.py:75
  81.5 4.3 all-to-all-start.9
  85.8 1.3 copy.163
  88.5 11.8 %all-to-all-done.9 = f32[2,4,128,256]{2,3,0,1:T(8,128)} async-done(((f32[2,4,128,256]{2,3,0,1:T(8,128)}), f32[2,4,128,256]{2,3,0,1:T(8,128)}, u32[]{:S(2)}, u32[]{:S(2)}) %all-to-all-start.9) | async-done | bytes 1048608 | tf_op jit(solution)/shard_map/all_to_all | solution.py:31
  100.3 3.4 all-to-all-start.3
  104.6 5.1 all-to-all-done.3
  109.6 1.6 stack.100
  111.3 3.6 all-to-all-start.1
  114.9 1.1 copy.136
  116.0 47.0 %all-to-all-done.1 = bf16[8,128,1024]{2,1,0:T(8,128)(2,1)S(1)} async-done(((bf16[8,128,1024]{2,1,0:T(8,128)(2,1)}), bf16[8,128,1024]{2,1,0:T(8,128)(2,1)S(1)}, u32[]{:S(2)}, u32[]{:S(2)}) %all-to-all-start.1) | async-done | bytes 2097184 | tf_op jit(solution)/shard_map/all_to_all | solution.py:17
  163.0 1.8 stack.102
  165.0 3.6 all-to-all-start.5
  168.6 1.1 copy.134
  170.6 46.4 %all-to-all-done.5 = bf16[8,128,1024]{2,1,0:T(8,128)(2,1)S(1)} async-done(((bf16[8,128,1024]{2,1,0:T(8,128)(2,1)}), bf16[8,128,1024]{2,1,0:T(8,128)(2,1)S(1)}, u32[]{:S(2)}, u32[]{:S(2)}) %all-to-all-start.5) | async-done | bytes 2097184 | tf_op jit(solution)/shard_map/all_to_all | solution.py:17
  217.0 2.7 stack.101
  219.7 3.6 all-to-all-start.4
  223.4 1.3 copy.162
  224.7 1.1 slice_multiply_fusion.1
  225.7 2.0 copy.155
  227.7 2.0 copy.156
  229.8 42.0 %all-to-all-done.4 = bf16[8,128,1024]{2,1,0:T(8,128)(2,1)S(1)} async-done(((bf16[8,128,1024]{2,1,0:T(8,128)(2,1)}), bf16[8,128,1024]{2,1,0:T(8,128)(2,1)S(1)}, u32[]{:S(2)}, u32[]{:S(2)}) %all-to-all-start.4) | async-done | bytes 2097184 | tf_op jit(solution)/shard_map/all_to_all | solution.py:17
  271.8 3.6 all-to-all-start.13
  275.4 3.4 fusion.53
  278.8 3.7 convolution_convert_fusion.2
  282.5 2.6 stack.114
  285.1 6.0 %all-to-all-start.10 = ((bf16[8,128,1024]{2,1,0:T(8,128)(2,1)}), bf16[8,128,1024]{2,1,0:T(8,128)(2,1)}, u32[]{:S(2)}, u32[]{:S(2)}) async-start(bf16[8,128,1024]{2,1,0:T(8,128)(2,1)} %stack.114), calls=%async_computation.10 | async-start | bytes 4194304 | tf_op jit(solution)/shard_map/all_to_all | solution.py:17
  292.2 1.2 copy.154
  293.4 1.2 fusion.51
  295.5 43.5 %all-to-all-done.10 = bf16[8,128,1024]{2,1,0:T(8,128)(2,1)} async-done(((bf16[8,128,1024]{2,1,0:T(8,128)(2,1)}), bf16[8,128,1024]{2,1,0:T(8,128)(2,1)}, u32[]{:S(2)}, u32[]{:S(2)}) %all-to-all-start.10) | async-done | bytes 2097184 | tf_op jit(solution)/shard_map/all_to_all | solution.py:17
  339.1 1.7 stack.109
  340.7 4.5 all-to-all-start.8
  348.4 44.7 %all-to-all-done.8 = bf16[8,128,1024]{2,1,0:T(8,128)(2,1)} async-done(((bf16[8,128,1024]{2,1,0:T(8,128)(2,1)}), bf16[8,128,1024]{2,1,0:T(8,128)(2,1)}, u32[]{:S(2)}, u32[]{:S(2)}) %all-to-all-start.8) | async-done | bytes 2097184 | tf_op jit(solution)/shard_map/all_to_all | solution.py:17
  393.0 1.6 stack.107
  394.6 3.9 all-to-all-start.7
  401.1 2.1 convolution_convert_fusion.1
  403.4 2.1 multiply_reduce_fusion
  405.5 3.5 fusion
  409.0 4.1 fusion.5
  413.1 1.1 stack.110
  414.3 32.6 %all-to-all-done.7 = bf16[8,128,1024]{2,1,0:T(8,128)(2,1)S(1)} async-done(((bf16[8,128,1024]{2,1,0:T(8,128)(2,1)}), bf16[8,128,1024]{2,1,0:T(8,128)(2,1)S(1)}, u32[]{:S(2)}, u32[]{:S(2)}) %all-to-all-start.7) | async-done | bytes 2097184 | tf_op jit(solution)/shard_map/all_to_all | solution.py:17
  446.9 3.6 all-to-all-start.14
  451.0 1.9 fusion.1
  452.9 3.4 fusion.4
  457.5 3.6 all-to-all-start.11
  462.8 9.9 %all-to-all-done.11 = bf16[3,4,128,256]{3,2,0,1:T(8,128)(2,1)S(1)} async-done(((bf16[3,4,128,256]{3,2,0,1:T(8,128)(2,1)}), bf16[3,4,128,256]{3,2,0,1:T(8,128)(2,1)S(1)}, u32[]{:S(2)}, u32[]{:S(2)}) %all-to-all-start.11) | async-done | bytes 786464 | tf_op jit(solution)/shard_map/all_to_all | solution.py:39
  472.7 3.5 all-to-all-start.6
  476.2 1.2 iota_compare_fusion.1
  477.4 1.3 iota_compare_fusion.3
  479.8 8.0 %all-to-all-done.6 = bf16[3,4,128,256]{3,2,0,1:T(8,128)(2,1)S(1)} async-done(((bf16[3,4,128,256]{3,2,0,1:T(8,128)(2,1)}), bf16[3,4,128,256]{3,2,0,1:T(8,128)(2,1)S(1)}, u32[]{:S(2)}, u32[]{:S(2)}) %all-to-all-start.6) | async-done | bytes 786464 | tf_op jit(solution)/shard_map/all_to_all | solution.py:39
  487.8 6.0 %all-to-all-start.12 = ((bf16[8,128,256]{2,1,0:T(8,128)(2,1)}), bf16[8,128,256]{2,1,0:T(8,128)(2,1)S(1)}, u32[]{:S(2)}, u32[]{:S(2)}) async-start(bf16[8,128,256]{2,1,0:T(8,128)(2,1)} %select_select_fusion), calls=%async_computation.12 | async-start | bytes 1048576 | tf_op jit(solution)/shard_map/all_to_all | solution.py:121
  493.9 3.2 fusion.14
  497.1 1.1 fusion.20
  498.2 9.8 %all-to-all-done.12 = bf16[8,128,256]{2,1,0:T(8,128)(2,1)S(1)} async-done(((bf16[8,128,256]{2,1,0:T(8,128)(2,1)}), bf16[8,128,256]{2,1,0:T(8,128)(2,1)S(1)}, u32[]{:S(2)}, u32[]{:S(2)}) %all-to-all-start.12) | async-done | bytes 524320 | tf_op jit(solution)/shard_map/all_to_all | solution.py:121
  (77 shorter events, 20.0 us)
Async XLA Ops:
  0.6 13.1 %copy-start = (bf16[1024,1024]{1,0:T(8,128)(2,1)S(1)}, bf16[1024,1024]{1,0:T(8,128)(2,1)}, u32[]{:S(2)}) copy-start(bf16[1024,1024]{1,0:T(8,128)(2,1)} %param.12) | copy-start | bytes 6291460
  0.7 3.8 copy-start.11
  7.4 18.7 %all-to-all-start = ((bf16[4,4,128,256]{2,3,0,1:T(8,128)(2,1)}), bf16[4,4,128,256]{2,3,0,1:T(8,128)(2,1)S(1)}, u32[]{:S(2)}, u32[]{:S(2)}) async-start(bf16[4,4,128,256]{2,3,0,1:T(8,128)(2,1)} %pad_maximum_fusion), calls=%async_computation | async-start | bytes 2097152 | tf_op jit(solution)/shard_map/all_to_all | solution.py:31
  26.1 1.0 copy-start.6
  27.0 54.4 %all-to-all-start.2 = ((bf16[8,128,1024]{2,1,0:T(8,128)(2,1)}), bf16[8,128,1024]{2,1,0:T(8,128)(2,1)S(1)}, u32[]{:S(2)}, u32[]{:S(2)}) async-start(bf16[8,128,1024]{2,1,0:T(8,128)(2,1)} %bitcast.139), calls=%async_computation.2 | async-start | bytes 4194304 | tf_op jit(solution)/shard_map/all_to_all | solution.py:75
  81.5 18.8 %all-to-all-start.9 = ((f32[2,4,128,256]{2,3,0,1:T(8,128)}), f32[2,4,128,256]{2,3,0,1:T(8,128)}, u32[]{:S(2)}, u32[]{:S(2)}) async-start(f32[2,4,128,256]{2,3,0,1:T(8,128)} %pad_maximum_fusion.1), calls=%async_computation.9 | async-start | bytes 2097152 | tf_op jit(solution)/shard_map/all_to_all | solution.py:31
  100.3 9.4 %all-to-all-start.3 = ((bf16[1,4,128,256]{3,2,0,1:T(8,128)(2,1)}), bf16[1,4,128,256]{3,2,0,1:T(8,128)(2,1)S(1)}, u32[]{:S(2)}, u32[]{:S(2)}) async-start(bf16[1,4,128,256]{3,2,0,1:T(8,128)(2,1)} %copy.133), calls=%async_computation.3 | async-start | bytes 524288 | tf_op jit(solution)/shard_map/all_to_all | solution.py:31
  104.4 6.8 %copy-start.7 = (bf16[1,128,4,256]{1,3,2,0:T(8,128)(2,1)}, bf16[1,128,4,256]{1,3,2,0:T(8,128)(2,1)S(1)}, u32[]{:S(2)}) copy-start(bf16[1,128,4,256]{1,3,2,0:T(8,128)(2,1)S(1)} %get-tuple-element.21) | copy-start | bytes 786436
  109.6 1.6 copy-start.13
  111.3 51.8 %all-to-all-start.1 = ((bf16[8,128,1024]{2,1,0:T(8,128)(2,1)}), bf16[8,128,1024]{2,1,0:T(8,128)(2,1)S(1)}, u32[]{:S(2)}, u32[]{:S(2)}) async-start(bf16[8,128,1024]{2,1,0:T(8,128)(2,1)} %stack.100), calls=%async_computation.1 | async-start | bytes 4194304 | tf_op jit(solution)/shard_map/all_to_all | solution.py:17
  163.0 2.0 copy-start.4
  165.0 52.0 %all-to-all-start.5 = ((bf16[8,128,1024]{2,1,0:T(8,128)(2,1)}), bf16[8,128,1024]{2,1,0:T(8,128)(2,1)S(1)}, u32[]{:S(2)}, u32[]{:S(2)}) async-start(bf16[8,128,1024]{2,1,0:T(8,128)(2,1)} %stack.102), calls=%async_computation.5 | async-start | bytes 4194304 | tf_op jit(solution)/shard_map/all_to_all | solution.py:17
  217.0 2.7 copy-start.2
  219.7 52.1 %all-to-all-start.4 = ((bf16[8,128,1024]{2,1,0:T(8,128)(2,1)}), bf16[8,128,1024]{2,1,0:T(8,128)(2,1)S(1)}, u32[]{:S(2)}, u32[]{:S(2)}) async-start(bf16[8,128,1024]{2,1,0:T(8,128)(2,1)} %stack.101), calls=%async_computation.4 | async-start | bytes 4194304 | tf_op jit(solution)/shard_map/all_to_all | solution.py:17
  271.8 10.7 %all-to-all-start.13 = ((f32[8,1,256]{2,1,0:T(1,128)}), f32[8,1,256]{2,1,0:T(1,128)S(1)}, u32[]{:S(2)}, u32[]{:S(2)}) async-start(f32[8,1,256]{2,1,0:T(1,128)} %bitcast.44), calls=%async_computation.13 | async-start | bytes 16384 | tf_op jit(solution)/shard_map/all_to_all | solution.py:124
  285.1 54.0 %all-to-all-start.10 = ((bf16[8,128,1024]{2,1,0:T(8,128)(2,1)}), bf16[8,128,1024]{2,1,0:T(8,128)(2,1)}, u32[]{:S(2)}, u32[]{:S(2)}) async-start(bf16[8,128,1024]{2,1,0:T(8,128)(2,1)} %stack.114), calls=%async_computation.10 | async-start | bytes 4194304 | tf_op jit(solution)/shard_map/all_to_all | solution.py:17
  293.4 1.7 copy-start.3
  340.7 4.5 copy-start.9
  340.7 52.3 %all-to-all-start.8 = ((bf16[8,128,1024]{2,1,0:T(8,128)(2,1)}), bf16[8,128,1024]{2,1,0:T(8,128)(2,1)}, u32[]{:S(2)}, u32[]{:S(2)}) async-start(bf16[8,128,1024]{2,1,0:T(8,128)(2,1)} %stack.109), calls=%async_computation.8 | async-start | bytes 4194304 | tf_op jit(solution)/shard_map/all_to_all | solution.py:17
  346.2 1.6 copy-start.5
  346.2 1.7 copy-start.10
  394.6 3.9 copy-start.15
  394.6 5.2 %copy-start.16 = (f32[256]{0:T(256)S(1)}, f32[256]{0:T(256)}, u32[]{:S(2)}) copy-start(f32[256]{0:T(256)} %param.23) | copy-start | bytes 3076
  394.6 5.2 %copy-start.17 = (f32[256]{0:T(256)S(1)}, f32[256]{0:T(256)}, u32[]{:S(2)}) copy-start(f32[256]{0:T(256)} %param.22) | copy-start | bytes 3076
  394.6 6.5 %copy-start.8 = (bf16[1,128,4,256]{1,3,2,0:T(8,128)(2,1)S(1)}, bf16[1,128,4,256]{1,3,2,0:T(8,128)(2,1)}, u32[]{:S(2)}) copy-start(bf16[1,128,4,256]{1,3,2,0:T(8,128)(2,1)} %copy-done.7) | copy-start | bytes 786436
  394.6 52.2 %all-to-all-start.7 = ((bf16[8,128,1024]{2,1,0:T(8,128)(2,1)}), bf16[8,128,1024]{2,1,0:T(8,128)(2,1)S(1)}, u32[]{:S(2)}, u32[]{:S(2)}) async-start(bf16[8,128,1024]{2,1,0:T(8,128)(2,1)} %stack.107), calls=%async_computation.7 | async-start | bytes 4194304 | tf_op jit(solution)/shard_map/all_to_all | solution.py:17
  446.9 10.6 %all-to-all-start.14 = ((f32[8,1,256]{2,1,0:T(1,128)}), f32[8,1,256]{2,1,0:T(1,128)S(1)}, u32[]{:S(2)}, u32[]{:S(2)}) async-start(f32[8,1,256]{2,1,0:T(1,128)} %broadcast_select_fusion), calls=%async_computation.14 | async-start | bytes 16384 | tf_op jit(solution)/shard_map/all_to_all | solution.py:131
  456.5 4.9 copy-start.12
  457.5 4.1 copy-start.14
  457.5 15.2 %all-to-all-start.11 = ((bf16[3,4,128,256]{3,2,0,1:T(8,128)(2,1)}), bf16[3,4,128,256]{3,2,0,1:T(8,128)(2,1)S(1)}, u32[]{:S(2)}, u32[]{:S(2)}) async-start(bf16[3,4,128,256]{3,2,0,1:T(8,128)(2,1)} %maximum_bitcast_fusion.1), calls=%async_computation.11 | async-start | bytes 1572864 | tf_op jit(solution)/shard_map/all_to_all | solution.py:39
  472.7 15.1 %all-to-all-start.6 = ((bf16[3,4,128,256]{3,2,0,1:T(8,128)(2,1)}), bf16[3,4,128,256]{3,2,0,1:T(8,128)(2,1)S(1)}, u32[]{:S(2)}, u32[]{:S(2)}) async-start(bf16[3,4,128,256]{3,2,0,1:T(8,128)(2,1)} %maximum_bitcast_fusion), calls=%async_computation.6 | async-start | bytes 1572864 | tf_op jit(solution)/shard_map/all_to_all | solution.py:39
  487.8 20.2 %all-to-all-start.12 = ((bf16[8,128,256]{2,1,0:T(8,128)(2,1)}), bf16[8,128,256]{2,1,0:T(8,128)(2,1)S(1)}, u32[]{:S(2)}, u32[]{:S(2)}) async-start(bf16[8,128,256]{2,1,0:T(8,128)(2,1)} %select_select_fusion), calls=%async_computation.12 | async-start | bytes 1048576 | tf_op jit(solution)/shard_map/all_to_all | solution.py:121
  493.9 15.5 %copy-start.1 = (bf16[1024,1024]{1,0:T(8,128)(2,1)S(1)}, bf16[1024,1024]{1,0:T(8,128)(2,1)}, u32[]{:S(2)}) copy-start(bf16[1024,1024]{1,0:T(8,128)(2,1)} %param.12) | copy-start | bytes 6291460
